TPU v7x, 256 devices: a whole 4x4x8 slice. The times are simulated.
256 devices in a mesh: group: 8 (over z), row: 32 (over y, x, core).
Axes of the slice: x: 4, y: 4, z: 8, core: 2. Of those that a mesh axis runs over, the one named last changes fastest.
Arguments:
- start_basis: float32 [2048, 16, 128], P(('group', 'row')), may hold values from -6 to 6
- tiles: bfloat16 [2048, 16, 128, 128], P(('group', 'row')), may hold values from -60000 to 60000
- tile_cols: int32 [2048, 16], P(('group', 'row')), may hold values from 0 to 75, as said below
- tile_count: int32 [2048], P(('group', 'row')), may hold values from 10 to 16, as said below
- recv_list: int32 [8, 32, 32, 2], P('group', 'row'), may hold values from -1 to 2047, as said below
Outputs:
- krylov: float32 [3, 2048, 16, 128], P(None, ('group', 'row'))
Inputs may be any that keep to these rules, and one draw needn't show every extreme that they name: For each reader device and each other device of its range, recv_list names distinct blocks of that peer in its first slots and -1 in the rest; a reader's own entry is all -1; every reader gets exactly 2 blocks from some peer. tile_cols never names an empty receive slot, nor a rim slot of a range that does not exist (before the first or after the last group); every filled receive slot and every existing rim slot is named by some tile slot below 10. `tile_count`: every device has a row block with all 16 tiles live.
All inputs are finite; a program needn't handle non-finite values.
Results may differ from a plain program's by a relative error of at most 0.0003.
Values sent between devices are 32-bit elements; how exact they have to be, the bound alone decides.
A program may use at most 64 MiB of HBM per device.

v0:
```python
import jax
import jax.numpy as jnp
from jax import lax
from jax.sharding import PartitionSpec as P

SLOTS = 2
RIM = 2
ITERS = 3


def padded(x, sides, width):
    for axis, dim in sides:
        count, length = (lax.axis_size(axis), x.shape[dim])
        up = [(i, (i + 1) % count) for i in range(count - 1)]
        down = [(j, i) for i, j in up]
        last = lax.slice_in_dim(x, length - width, length, axis=dim)
        leading = lax.slice_in_dim(x, 0, width, axis=dim)
        before = lax.ppermute(last, axis, up)
        after = lax.ppermute(leading, axis, down)
        x = jnp.concatenate([before, x, after], axis=dim)
    return x


def orthonormal(applied, gram_sum, row_total):
    vectors = applied.shape[1]
    factor = jnp.linalg.cholesky(gram_sum / row_total)
    inverse = lax.linalg.triangular_solve(
        factor, jnp.eye(vectors, dtype=jnp.float32), left_side=True, lower=True
    )
    return jnp.einsum("kl,bli->bki", inverse, applied, precision=lax.Precision.HIGHEST)


def local(start_basis, tiles, tile_cols, tile_count, recv_list):
    groups = lax.axis_size("group")
    peers = lax.axis_size("row")
    group_at = lax.axis_index("group")
    blocks = tiles.shape[0]
    per_row = tiles.shape[1]
    tile_side = tiles.shape[2]
    row_total = groups * peers * blocks * tile_side
    live_mask = (jnp.arange(per_row, dtype=jnp.int32)[None, :] < tile_count[:, None]).astype(
        jnp.float32
    )
    wide_tiles = tiles.astype(jnp.float32)
    sum_sq = jnp.einsum(
        "btij,bt->bi", wide_tiles * wide_tiles, live_mask, precision=lax.Precision.HIGHEST
    )
    inv_root = (1e-06 + sum_sq) ** (-0.25)
    wanted = recv_list.reshape(peers, SLOTS)
    gather_pick = jnp.clip(wanted - group_at * peers * blocks, 0, peers * blocks - 1).reshape(-1)
    results = []
    basis = start_basis
    for step_at in range(ITERS):
        scaled = basis * inv_root[:, None, :]
        rimmed = padded(scaled, (("group", 0),), RIM)
        group_all = lax.all_gather(scaled, "row", axis=0, tiled=True)
        received = jnp.take(group_all, gather_pick, axis=0)
        extended = jnp.concatenate([scaled, received, rimmed[:RIM], rimmed[blocks + RIM :]], axis=0)
        picked = jnp.take(extended, tile_cols, axis=0) * live_mask[:, :, None, None]
        product = jnp.einsum(
            "btij,btkj->bki",
            tiles,
            picked,
            precision=lax.Precision.HIGHEST,
            preferred_element_type=jnp.float32,
        )
        applied = product * inv_root[:, None, :]
        partial_value = jnp.einsum("bki,bli->kl", applied, applied, precision=lax.Precision.HIGHEST)
        gram_sum = lax.psum(partial_value, ("group", "row"))
        basis = orthonormal(applied, gram_sum, row_total)
        results.append(basis)
    return jnp.stack(results)


def solution(mesh):
    placed = (
        P(("group", "row"), None, None),
        P(("group", "row"), None, None, None),
        P(("group", "row"), None),
        P(("group", "row")),
        P("group", "row", None, None),
    )
    return jax.shard_map(
        local,
        mesh=mesh,
        in_specs=placed,
        out_specs=P(None, ("group", "row"), None, None),
        check_vma=False,
    )
```

profile of v0, /device:TPU:1, one launch (start us, length us, event | category | flops | bytes accessed | tf_op | source)
XLA Modules:
  0.0 434.7 jit_solution(10057653734697218750)
XLA Ops:
  6.6 4.5 %multiply_reduce_fusion = f32[8,16,128]{2,1,0:T(8,128)S(1)} fusion(bf16[8,16,128,128]{3,2,1,0:T(8,128)(2,1)} %param.13), kind=kLoop, calls=%fused_computation.6 | loop fusion | flops 6275072 | bytes 4259840 | tf_op jit(solution)/shard_map/btij,bt->bi/reduce_sum | solution.py:45
  11.3 0.6 broadcast_multiply_fusion
  12.0 0.7 fusion.33
  12.8 4.4 %collective-permute-start = (f32[2,16,128]{2,1,0:T(8,128)S(1)}, f32[2,16,128]{2,1,0:T(8,128)S(1)}, u32[]{:S(2)}, u32[]{:S(2)}) collective-permute-start(f32[2,16,128]{2,1,0:T(8,128)S(1)} %get-tuple-element.13), channel_id=1, source_target_pairs={{0,32},{32,64},{64,96},{96,128},{128,160},{160,192},{192,224},{1,3... | collective-permute-start | bytes 49160 | tf_op jit(solution)/shard_map/ppermute | solution.py:18
  17.2 1.3 collective-permute-start.1
  18.8 46.4 %all-gather.4.cloned.1.call-done = f32[256,16,128]{2,1,0:T(8,128)} async-done(((f32[8,16,128]{2,1,0:T(8,128)}), f32[256,16,128]{2,1,0:T(8,128)}) %all-gather.4.cloned.1.call-update) | async-done | bytes 2097168 | tf_op jit(solution)/shard_map/all_gather | solution.py:56
  65.2 2.2 gather_fusion
  67.6 0.9 pad_maximum_fusion
  68.5 0.8 gather_fusion.1
  69.2 5.2 %fusion.2 = f32[8,16,128]{2,1,0:T(8,128)S(1)} fusion(bf16[8,16,128,128]{3,2,1,0:T(8,128)(2,1)} %param.13, f32[8,16,16,128]{3,2,1,0:T(8,128)S(1)} %bitcast.92, f32[8,16]{1,0:T(8,128)S(1)} %get-tuple-element.15, pred[8,16]{1,0:T(8,128)(4,1)S(1)} %get-tuple-element.21, f32[8,128]{1,0:T(8,128)S(1)} %add_power_fusion), kind=kOutput, calls=%fused_computation.13 | convolution fusion | flops 403193856 | bytes 5313152 | tf_op jit(solution)/shard_map/btij,btkj->bki/dot_general | solution.py:60
  74.6 75.6 %psum.21 = f32[16,16]{0,1:T(8,128)S(1)} all-reduce(f32[16,16]{0,1:T(8,128)S(1)} %convolution_bitcast_fusion.9), channel_id=1, replica_groups=mesh['group'=8,'row'=32] {'group','row'}, use_global_device_ids=true, to_apply=%region_1.0 | all-reduce | flops 256 | bytes 2048 | tf_op jit(solution)/shard_map/psum | solution.py:69
  150.3 1.5 cholesky.59
  151.7 0.6 compare_reduce_fusion.2
  152.4 0.6 fusion.17
  153.0 1.2 custom-call.7
  154.3 0.2 convolution_bitcast_fusion.8
  154.5 0.8 bitcast_multiply_fusion.1
  155.4 0.7 fusion.32
  156.1 2.9 collective-permute-start.2
  159.1 1.3 collective-permute-start.3
  160.4 41.2 %all-gather.6.cloned.1.call-done = f32[256,16,128]{2,1,0:T(8,128)} async-done(((f32[8,16,128]{2,1,0:T(8,128)}), f32[256,16,128]{2,1,0:T(8,128)}) %all-gather.6.cloned.1.call-update) | async-done | bytes 2097168 | tf_op jit(solution)/shard_map/all_gather | solution.py:56
  201.6 2.2 gather_fusion.2
  204.0 0.9 pad_maximum_fusion.1
  204.9 0.8 gather_fusion.3
  205.6 5.2 %fusion.1 = f32[8,16,128]{2,1,0:T(8,128)S(1)} fusion(bf16[8,16,128,128]{3,2,1,0:T(8,128)(2,1)} %param.13, f32[8,16,16,128]{3,2,1,0:T(8,128)S(1)} %bitcast.93, f32[8,16]{1,0:T(8,128)S(1)} %get-tuple-element.15, pred[8,16]{1,0:T(8,128)(4,1)S(1)} %get-tuple-element.21, f32[8,128]{1,0:T(8,128)S(1)} %add_power_fusion), kind=kOutput, calls=%fused_computation.11 | convolution fusion | flops 403193856 | bytes 5313152 | tf_op jit(solution)/shard_map/btij,btkj->bki/dot_general | solution.py:60
  211.0 75.6 %psum.22 = f32[16,16]{0,1:T(8,128)S(1)} all-reduce(f32[16,16]{0,1:T(8,128)S(1)} %convolution_bitcast_fusion.7), channel_id=1, replica_groups=mesh['group'=8,'row'=32] {'group','row'}, use_global_device_ids=true, to_apply=%region_4.9 | all-reduce | flops 256 | bytes 2048 | tf_op jit(solution)/shard_map/psum | solution.py:69
  286.6 1.5 cholesky.70
  288.1 0.6 compare_reduce_fusion.1
  288.8 0.6 fusion.18
  289.4 1.2 custom-call.8
  290.7 0.2 convolution_bitcast_fusion.6
  290.9 0.8 bitcast_multiply_fusion
  291.7 0.7 fusion.31
  292.5 2.9 collective-permute-start.4
  295.4 1.3 collective-permute-start.5
  296.7 41.3 %all-gather.8.cloned.1.call-done = f32[256,16,128]{2,1,0:T(8,128)} async-done(((f32[8,16,128]{2,1,0:T(8,128)}), f32[256,16,128]{2,1,0:T(8,128)}) %all-gather.8.cloned.1.call-update) | async-done | bytes 2097168 | tf_op jit(solution)/shard_map/all_gather | solution.py:56
  338.0 2.2 gather_fusion.4
  340.4 0.9 pad_maximum_fusion.2
  341.2 0.8 gather_fusion.5
  342.0 5.2 %fusion = f32[8,16,128]{2,1,0:T(8,128)S(1)} fusion(bf16[8,16,128,128]{3,2,1,0:T(8,128)(2,1)} %param.13, f32[8,16,16,128]{3,2,1,0:T(8,128)S(1)} %bitcast.91, f32[8,16]{1,0:T(8,128)S(1)} %get-tuple-element.15, pred[8,16]{1,0:T(8,128)(4,1)S(1)} %get-tuple-element.21, f32[8,128]{1,0:T(8,128)S(1)} %add_power_fusion), kind=kOutput, calls=%fused_computation.9 | convolution fusion | flops 403193856 | bytes 5313152 | tf_op jit(solution)/shard_map/btij,btkj->bki/dot_general | solution.py:60
  347.4 75.6 %psum.23 = f32[16,16]{0,1:T(8,128)S(1)} all-reduce(f32[16,16]{0,1:T(8,128)S(1)} %convolution_bitcast_fusion.5), channel_id=1, replica_groups=mesh['group'=8,'row'=32] {'group','row'}, use_global_device_ids=true, to_apply=%region_5.10 | all-reduce | flops 256 | bytes 2048 | tf_op jit(solution)/shard_map/psum | solution.py:69
  423.0 1.5 cholesky.81
  424.5 0.6 compare_reduce_fusion
  425.2 0.6 fusion.19
  425.8 1.2 custom-call.9
  427.0 0.2 convolution_bitcast_fusion.4
  427.2 0.2 convolution_bitcast_fusion
  427.5 0.7 pad_maximum_fusion.3
  (50 shorter events, 2.0 us)
Async XLA Ops:
  6.5 4.5 %copy-start.1 = (s32[8,16]{1,0:T(8,128)S(1)}, s32[8,16]{1,0:T(8,128)}, u32[]{:S(2)}) copy-start(s32[8,16]{1,0:T(8,128)} %param.14) | copy-start | bytes 1540
  6.5 4.5 %copy-start.3 = (s32[8]{0:T(128)S(1)}, s32[8]{0:T(128)}, u32[]{:S(2)}) copy-start(s32[8]{0:T(128)} %param.15) | copy-start | bytes 100
  6.5 4.8 %copy-start = (f32[8,16,128]{2,1,0:T(8,128)S(1)}, f32[8,16,128]{2,1,0:T(8,128)}, u32[]{:S(2)}) copy-start(f32[8,16,128]{2,1,0:T(8,128)} %param.12) | copy-start | bytes 196612
  6.5 12.0 %copy-start.2 = (s32[1,1,32,2]{2,3,1,0:T(2,128)S(1)}, s32[1,1,32,2]{2,3,1,0:T(2,128)}, u32[]{:S(2)}) copy-start(s32[1,1,32,2]{2,3,1,0:T(2,128)} %param.16) | copy-start | bytes 772
  6.5 58.7 %all-gather.4.cloned.1.call-start = ((), (), s32[]{:S(2)}) async-start(), calls=%async_computation | async-start | bytes 2162688 | tf_op jit(solution)/shard_map/all_gather | solution.py:56
  12.0 189.6 %all-gather.6.cloned.1.call-start = ((), (), s32[]{:S(2)}) async-start(), calls=%async_computation.1 | async-start | bytes 2162688 | tf_op jit(solution)/shard_map/all_gather | solution.py:56
  12.8 54.8 %collective-permute-start = (f32[2,16,128]{2,1,0:T(8,128)S(1)}, f32[2,16,128]{2,1,0:T(8,128)S(1)}, u32[]{:S(2)}, u32[]{:S(2)}) collective-permute-start(f32[2,16,128]{2,1,0:T(8,128)S(1)} %get-tuple-element.13), channel_id=1, source_target_pairs={{0,32},{32,64},{64,96},{96,128},{128,160},{160,192},{192,224},{1,3... | collective-permute-start | bytes 49160 | tf_op jit(solution)/shard_map/ppermute | solution.py:18
  17.2 50.4 %collective-permute-start.1 = (f32[2,16,128]{2,1,0:T(8,128)S(1)}, f32[2,16,128]{2,1,0:T(8,128)S(1)}, u32[]{:S(2)}, u32[]{:S(2)}) collective-permute-start(f32[2,16,128]{2,1,0:T(8,128)S(1)} %get-tuple-element.14), channel_id=1, source_target_pairs={{32,0},{64,32},{96,64},{128,96},{160,128},{192,160},{224,192},{33,... | collective-permute-start | bytes 49160 | tf_op jit(solution)/shard_map/ppermute | solution.py:19
  155.3 182.7 %all-gather.8.cloned.1.call-start = ((), (), s32[]{:S(2)}) async-start(), calls=%async_computation.2 | async-start | bytes 2162688 | tf_op jit(solution)/shard_map/all_gather | solution.py:56
  156.1 47.8 %collective-permute-start.2 = (f32[2,16,128]{2,1,0:T(8,128)S(1)}, f32[2,16,128]{2,1,0:T(8,128)S(1)}, u32[]{:S(2)}, u32[]{:S(2)}) collective-permute-start(f32[2,16,128]{2,1,0:T(8,128)S(1)} %get-tuple-element.10), channel_id=1, source_target_pairs={{0,32},{32,64},{64,96},{96,128},{128,160},{160,192},{192,224},{1,3... | collective-permute-start | bytes 49160 | tf_op jit(solution)/shard_map/ppermute | solution.py:18
  159.1 44.9 %collective-permute-start.3 = (f32[2,16,128]{2,1,0:T(8,128)S(1)}, f32[2,16,128]{2,1,0:T(8,128)S(1)}, u32[]{:S(2)}, u32[]{:S(2)}) collective-permute-start(f32[2,16,128]{2,1,0:T(8,128)S(1)} %get-tuple-element.12), channel_id=1, source_target_pairs={{32,0},{64,32},{96,64},{128,96},{160,128},{192,160},{224,192},{33,... | collective-permute-start | bytes 49160 | tf_op jit(solution)/shard_map/ppermute | solution.py:19
  292.5 47.9 %collective-permute-start.4 = (f32[2,16,128]{2,1,0:T(8,128)S(1)}, f32[2,16,128]{2,1,0:T(8,128)S(1)}, u32[]{:S(2)}, u32[]{:S(2)}) collective-permute-start(f32[2,16,128]{2,1,0:T(8,128)S(1)} %get-tuple-element.6), channel_id=1, source_target_pairs={{0,32},{32,64},{64,96},{96,128},{128,160},{160,192},{192,224},{1,3... | collective-permute-start | bytes 49160 | tf_op jit(solution)/shard_map/ppermute | solution.py:18
  295.4 44.9 %collective-permute-start.5 = (f32[2,16,128]{2,1,0:T(8,128)S(1)}, f32[2,16,128]{2,1,0:T(8,128)S(1)}, u32[]{:S(2)}, u32[]{:S(2)}) collective-permute-start(f32[2,16,128]{2,1,0:T(8,128)S(1)} %get-tuple-element.8), channel_id=1, source_target_pairs={{32,0},{64,32},{96,64},{128,96},{160,128},{192,160},{224,192},{33,... | collective-permute-start | bytes 49160 | tf_op jit(solution)/shard_map/ppermute | solution.py:19
Sparse Core Ops, SparseCore 0:
  12.1 53.0 all-gather.3
  155.5 46.1 all-gather.5
  291.8 46.1 all-gather.7
where the time goes:
time: 436 us; the launch traced here: 435 us
  blocking collectives  227 us (52%)
  waiting for transfers between devices  129 us (30%)
  other arithmetic  21 us (5%)
  matrix products  18.7 us (4%)
  starting transfers between devices  14.2 us (3%)
  between operations  13.4 us (3%)
  local copies, waits for them, and re-layouts  11.6 us (3%)
    psum x3, blocking collectives, local(): gram_sum = lax.psum(partial_value, ('group', 'row'))  227 us
    all_gather x3, waiting for transfers between devices, local(): group_all = lax.all_gather(scaled, 'row', axis=0, tiled=True)  129 us
    dot_general x3, matrix products, local(): jnp.einsum('btij,btkj->bki', tiles, picked, precision=lax.Precision.HIGHE...  15.5 us
    ppermute x3, starting transfers between devices, padded(): before = lax.ppermute(last, axis, up)  10.2 us
  transfers between devices with their start and end apart: 9, of which 3 were waited for; matrix products, arithmetic and copies ran while one was open for 2% of the time, Pallas kernels for 0%

commit v1 on v0

v1 whole, which is shorter than its diff:
```python
import functools

import jax
import jax.numpy as jnp
from jax import lax
from jax.experimental import pallas as pl
from jax.experimental.pallas import tpu as pltpu
from jax.sharding import PartitionSpec as P

SLOTS = 2
RIM = 2
ITERS = 3
MINLIVE = 10
MESH = pl.DeviceIdType.MESH
F32 = jnp.float32
BF16 = jnp.bfloat16
HIGHEST = lax.Precision.HIGHEST
NT = (((1,), (1,)), ((), ()))


def split(x):
    high = x.astype(BF16)
    return high, (x - high.astype(F32)).astype(BF16)


def kernel(
    groups,
    peers,
    cols,
    count,
    wanted,
    basis,
    tiles_hbm,
    out,
    tiles,
    inv_root,
    applied,
    own_0,
    own_1,
    own_2,
    stage,
    recv_0,
    recv_1,
    recv_2,
    rim,
    pieces,
    table,
    table_s,
    gram_near_0,
    gram_near_1,
    gram_near_2,
    gram_far_0,
    gram_far_1,
    gram_far_2,
    tile_sem,
    table_sem,
    list_sem,
    send_sem,
    recv_sem,
    rim_send,
    rim_recv,
    near_send,
    near_recv,
    far_send,
    far_recv,
):
    blocks, vectors, side = basis.shape
    per_row = cols.shape[1]
    own = (own_0, own_1, own_2)
    recv = (recv_0, recv_1, recv_2)
    gram_near = (gram_near_0, gram_near_1, gram_near_2)
    gram_far = (gram_far_0, gram_far_1, gram_far_2)
    group = lax.axis_index("group")
    me = lax.axis_index("row")
    up = lax.rem(group + 1, groups)
    down = lax.rem(group + groups - 1, groups)
    zero_slot = blocks + SLOTS * peers + 2 * RIM

    def peer(step):
        return lax.rem(me + step, peers)

    def far_peer(step):
        return lax.rem(group + step, groups)

    def copy_in(b):
        return pltpu.make_async_copy(tiles_hbm.at[b], tiles.at[b], tile_sem.at[b])

    for b in range(blocks):
        copy_in(b).start()

    barrier = pltpu.get_barrier_semaphore()

    @pl.loop(1, peers)
    def _(step):
        pl.semaphore_signal(barrier, inc=1, device_id=(group, peer(step)), device_id_type=MESH)

    @pl.loop(1, groups)
    def _(step):
        pl.semaphore_signal(barrier, inc=1, device_id=(far_peer(step), me), device_id_type=MESH)

    pl.semaphore_wait(barrier, peers - 1 + groups - 1)

    @pl.loop(1, peers)
    def _(step):
        pltpu.make_async_remote_copy(
            src_ref=wanted,
            dst_ref=table.at[me],
            send_sem=list_sem.at[0],
            recv_sem=list_sem.at[1],
            device_id=(group, peer(step)),
            device_id_type=MESH,
        ).start()

    ones = jnp.ones((vectors, 2 * side), BF16)

    @pl.loop(0, blocks)
    def _(b):
        copy_in(b).wait()
        live = count[b]
        total = jnp.zeros((side, side), F32)
        for s in range(per_row):
            wide = tiles[b, s].astype(F32)
            square = wide * wide
            if s >= MINLIVE:
                square = square * jnp.where(s < live, 1.0, 0.0).astype(F32)
            total = total + square
        sums = lax.dot_general(
            ones, jnp.concatenate(split(total), axis=1), NT, preferred_element_type=F32
        )
        root = 1.0 / jnp.sqrt(jnp.sqrt(1e-06 + sums))
        inv_root[b] = root
        own_0[b] = basis[b] * root

    def list_wait(ref, sem):
        return pltpu.make_async_copy(ref, ref, sem)

    part = table.at[pl.ds(0, peers - 1)]
    list_wait(part, list_sem.at[0]).wait()
    list_wait(part, list_sem.at[1]).wait()
    to_scalar = pltpu.make_async_copy(table, table_s, table_sem)
    to_scalar.start()
    to_scalar.wait()

    first_block = (group * peers + me) * blocks

    def send(t):
        source = own[t]
        for at, (lo, target) in enumerate(((blocks - RIM, up), (0, down))):
            pltpu.make_async_remote_copy(
                src_ref=source.at[pl.ds(lo, RIM)],
                dst_ref=rim.at[t, at],
                send_sem=rim_send.at[t, at],
                recv_sem=rim_recv.at[t, at],
                device_id=(target, me),
                device_id_type=MESH,
            ).start()

        @pl.loop(1, peers)
        def _(step):
            q = peer(step)
            for c in range(SLOTS):
                pick = jnp.clip(table_s[q, c, me] - first_block, 0, blocks - 1)
                stage[t, q, c] = source[pick]
            pltpu.make_async_remote_copy(
                src_ref=stage.at[t, q],
                dst_ref=recv[t].at[me],
                send_sem=send_sem.at[t],
                recv_sem=recv_sem.at[t],
                device_id=(group, q),
                device_id_type=MESH,
            ).start()

    def wait_recv(t):
        part = recv[t].at[pl.ds(0, peers - 1)]
        list_wait(part, recv_sem.at[t]).wait()
        for at in range(2):
            list_wait(rim.at[t, at], rim_recv.at[t, at]).wait()

    def put_pieces(at, value):
        high, low = split(value)
        pieces[pl.ds(at, value.shape[0]), 0:vectors] = high
        pieces[pl.ds(at, value.shape[0]), vectors : 2 * vectors] = low

    def multiply(t):
        put_pieces(0, own[t][...])

        @pl.loop(0, peers)
        def _(q):
            put_pieces(blocks + SLOTS * q, recv[t][q])

        for at in range(2):
            put_pieces(blocks + SLOTS * peers + RIM * at, rim[t, at])

        @pl.loop(0, blocks)
        def _(b):
            live = count[b]
            picked = []
            for s in range(per_row):
                slot = cols[b, s]
                if s >= MINLIVE:
                    slot = jnp.where(s < live, slot, zero_slot)
                picked.append(pieces[slot])
            both = lax.dot_general(
                jnp.concatenate(picked, axis=1),
                jnp.concatenate([tiles[b, s] for s in range(per_row)], axis=1),
                NT,
                preferred_element_type=F32,
            )
            applied[b] = (both[:vectors] + both[vectors:]) * inv_root[b]

    def wide(ref):
        return jnp.concatenate([ref[b] for b in range(blocks)], axis=1)

    row_of = lax.broadcasted_iota(jnp.int32, (vectors, side), 0)
    lane_of = lax.broadcasted_iota(jnp.int32, (vectors, side), 1)
    own_lane = lax.rem(row_of, 8) == lane_of // vectors
    row_total = groups * peers * blocks * side

    def gram_start(t, value):
        gram = lax.dot_general(
            value,
            jnp.concatenate([value] * (side // vectors), axis=0),
            NT,
            precision=HIGHEST,
            preferred_element_type=F32,
        )
        packed = jnp.sum(jnp.where(own_lane, gram, 0.0).reshape(vectors // 8, 8, side), axis=1)
        gram_near[t][me] = packed

        @pl.loop(1, peers)
        def _(step):
            pltpu.make_async_remote_copy(
                src_ref=gram_near[t].at[me],
                dst_ref=gram_near[t].at[me],
                send_sem=near_send.at[t],
                recv_sem=near_recv.at[t],
                device_id=(group, peer(step)),
                device_id_type=MESH,
            ).start()

    def gram_far_start(t):
        list_wait(gram_near[t].at[pl.ds(0, peers - 1)], near_recv.at[t]).wait()
        gram_far[t][group] = jnp.sum(gram_near[t][...], axis=0)

        @pl.loop(1, groups)
        def _(step):
            pltpu.make_async_remote_copy(
                src_ref=gram_far[t].at[group],
                dst_ref=gram_far[t].at[group],
                send_sem=far_send.at[t],
                recv_sem=far_recv.at[t],
                device_id=(far_peer(step), me),
                device_id_type=MESH,
            ).start()

    def gram_end(t):
        list_wait(gram_far[t].at[pl.ds(0, groups - 1)], far_recv.at[t]).wait()
        packed = jnp.sum(gram_far[t][...], axis=0) / row_total
        rows = jnp.broadcast_to(packed[:, None, :], (vectors // 8, 8, side)).reshape(vectors, side)
        full = jnp.where(own_lane, rows, 0.0)
        for shift in (64, 32, 16):
            full = full + pltpu.roll(full, shift, 1)
        both = jnp.where(lane_of < vectors, jnp.where(lane_of == row_of, 1.0, 0.0), full)
        pivots = jnp.zeros((vectors, side), F32)
        for j in range(vectors):
            pivot_row = jnp.broadcast_to(both[j : j + 1], (vectors, side))
            column = jnp.broadcast_to(both[:, vectors + j : vectors + j + 1], (vectors, side))
            pivot = jnp.broadcast_to(pivot_row[:, vectors + j : vectors + j + 1], (vectors, side))
            pivots = jnp.where(row_of == j, pivot, pivots)
            both = jnp.where(row_of > j, both - (column / pivot) * pivot_row, both)
        return (both / jnp.sqrt(pivots))[:, :vectors]

    def normalise(inverse, value):
        return lax.dot_general(
            inverse,
            value,
            (((1,), (0,)), ((), ())),
            precision=HIGHEST,
            preferred_element_type=F32,
        )

    def store_out(t, value):
        for b in range(blocks):
            out[t, b] = value[:, b * side : (b + 1) * side]

    pieces[zero_slot] = jnp.zeros((2 * vectors, side), BF16)
    send(0)
    wait_recv(0)
    multiply(0)
    current = wide(applied)
    for t in range(ITERS):
        if t + 1 < ITERS:
            for b in range(blocks):
                own[t + 1][b] = current[:, b * side : (b + 1) * side] * inv_root[b]
        gram_start(t, current)
        if t + 1 < ITERS:
            send(t + 1)
        gram_far_start(t)
        inverse = gram_end(t)
        store_out(t, normalise(inverse, current))
        if t + 1 < ITERS:
            wait_recv(t + 1)
            multiply(t + 1)
            current = normalise(inverse, wide(applied))

    for t in range(ITERS):
        list_wait(stage.at[t, pl.ds(0, peers - 1)], send_sem.at[t]).wait()
        for at in range(2):
            list_wait(rim.at[t, at], rim_send.at[t, at]).wait()
        list_wait(gram_near[t].at[pl.ds(0, peers - 1)], near_send.at[t]).wait()
        list_wait(gram_far[t].at[pl.ds(0, groups - 1)], far_send.at[t]).wait()


def local(groups, peers, start_basis, tiles, tile_cols, tile_count, recv_list):
    blocks, per_row, side, _ = tiles.shape
    vectors = start_basis.shape[1]
    wanted = jnp.transpose(recv_list.reshape(peers, SLOTS))
    slots = blocks + SLOTS * peers + 2 * RIM + 1
    dma = pltpu.SemaphoreType.DMA
    vmem = pltpu.VMEM
    smem = pl.BlockSpec(memory_space=pltpu.SMEM)
    near = vmem((peers, vectors // 8, side), F32)
    far = vmem((groups, vectors // 8, side), F32)
    return pl.pallas_call(
        functools.partial(kernel, groups, peers),
        out_shape=jax.ShapeDtypeStruct((ITERS, blocks, vectors, side), F32),
        in_specs=[
            smem,
            smem,
            pl.BlockSpec(memory_space=pltpu.VMEM),
            pl.BlockSpec(memory_space=pltpu.VMEM),
            pl.BlockSpec(memory_space=pl.ANY),
        ],
        out_specs=pl.BlockSpec(memory_space=pltpu.VMEM),
        scratch_shapes=[
            vmem((blocks, per_row, side, side), BF16),
            vmem((blocks, vectors, side), F32),
            vmem((blocks, vectors, side), F32),
        ]
        + [vmem((blocks, vectors, side), F32)] * ITERS
        + [vmem((ITERS, peers, SLOTS, vectors, side), F32)]
        + [vmem((peers, SLOTS, vectors, side), F32)] * ITERS
        + [
            vmem((ITERS, 2, RIM, vectors, side), F32),
            vmem((slots, 2 * vectors, side), BF16),
            vmem((peers, SLOTS, peers), jnp.int32),
            pltpu.SMEM((peers, SLOTS, peers), jnp.int32),
        ]
        + [near] * ITERS
        + [far] * ITERS
        + [
            dma((blocks,)),
            dma,
            dma((2,)),
            dma((ITERS,)),
            dma((ITERS,)),
            dma((ITERS, 2)),
            dma((ITERS, 2)),
            dma((ITERS,)),
            dma((ITERS,)),
            dma((ITERS,)),
            dma((ITERS,)),
        ],
        compiler_params=pltpu.CompilerParams(
            collective_id=0, has_side_effects=True, vmem_limit_bytes=40 << 20
        ),
    )(tile_cols, tile_count, wanted, start_basis, tiles)


def solution(mesh):
    placed = (
        P(("group", "row"), None, None),
        P(("group", "row"), None, None, None),
        P(("group", "row"), None),
        P(("group", "row")),
        P("group", "row", None, None),
    )
    return jax.shard_map(
        functools.partial(local, mesh.shape["group"], mesh.shape["row"]),
        mesh=mesh,
        in_specs=placed,
        out_specs=P(None, ("group", "row"), None, None),
        check_vma=False,
    )
```

time: 436 us -> 77.8 us (0.18)
  blocking collectives: 227 us -> 0 us
  waiting for transfers between devices: 129 us -> 0 us
  Pallas kernels: 0 us -> 71.9 us
  other arithmetic: 21 us -> 0 us
  matrix products: 18.7 us -> 0 us
  starting transfers between devices: 14.2 us -> 0 us
  between operations: 13.4 us -> 0.01 us
  local copies, waits for them, and re-layouts: 11.6 us -> 5.73 us
    psum x3 -> x0, blocking collectives: 227 us -> none  [local(): gram_sum = lax.psum(partial_value, ('group', 'row'))]
    all_gather x3 -> x0, waiting for transfers between devices: 129 us -> none  [local(): group_all = lax.all_gather(scaled, 'row', axis=0, tiled=True)]
    pallas_call x0 -> x1, Pallas kernels: none -> 71.9 us  [local(): pl.pallas_call(functools.partial(kernel, groups, peers), out_shape=jax.Sh...]
    dot_general x10 -> x0, matrix products: 18.1 us -> none  [the longest x3 15.5 us: local(): jnp.einsum('btij,btkj->bki', tiles, picked, precision=lax.Precision.HIGHE...]
    ppermute x6 -> x0, starting transfers between devices: 14.1 us -> none  [the longest x3 10.2 us: padded(): before = lax.ppermute(last, axis, up)]
    another operation x16 -> x0, other arithmetic: 12.7 us -> none  [the longest x9 6.39 us: orthonormal(): factor = jnp.linalg.cholesky(gram_sum / row_total)]
    gather x6 -> x0, local copies, waits for them, and re-layouts: 8.83 us -> none  [the longest x3 6.55 us: local(): received = jnp.take(group_all, gather_pick, axis=0)]
    unnamed x8 -> x11, local copies, waits for them, and re-layouts: 0.01 us -> 5.73 us
  transfers between devices with their start and end apart: 9 -> 0, of which waited for: 3 -> 0; matrix products, arithmetic and copies ran while one was open for 2% -> 0% of each run, Pallas kernels for 0% -> 0%
where the time goes in v1:
time: 77.8 us; the launch traced here: 77.6 us
  Pallas kernels  71.9 us (92%)
  local copies, waits for them, and re-layouts  5.73 us (7%)
    pallas_call x1, Pallas kernels, local(): pl.pallas_call(functools.partial(kernel, groups, peers), out_shape=jax.Sh...  71.9 us
    unnamed x11, local copies, waits for them, and re-layouts  5.73 us

profile of v1, /device:TPU:1, one launch (start us, length us, event | category | flops | bytes accessed | tf_op | source)
XLA Modules:
  0.0 77.6 jit_solution(8917612747424261407)
XLA Ops:
  0.0 0.0 copy-start
  0.0 2.2 %copy-done = bf16[8,16,128,128]{3,2,1,0:T(8,128)(2,1)S(1)} copy-done((bf16[8,16,128,128]{3,2,1,0:T(8,128)(2,1)S(1)}, bf16[8,16,128,128]{3,2,1,0:T(8,128)(2,1)}, u32[]{:S(2)}) %copy-start) | copy-done | bytes 4194328
  2.2 0.0 copy-start.1
  2.2 0.8 %copy-done.1 = f32[8,16,128]{2,1,0:T(8,128)S(1)} copy-done((f32[8,16,128]{2,1,0:T(8,128)S(1)}, f32[8,16,128]{2,1,0:T(8,128)}, u32[]{:S(2)}) %copy-start.1) | copy-done | bytes 65560
  3.0 0.0 copy-start.2
  3.0 0.7 copy-done.2
  3.7 0.0 copy-start.3
  3.7 0.7 copy-done.3
  4.4 0.0 copy-start.4
  4.4 0.7 copy-done.4
  5.1 71.9 %shard_map.55 = f32[3,8,16,128]{3,2,1,0:T(8,128)S(1)} custom-call(s32[8,16]{1,0:T(8,128)S(1)} %copy-done.2, s32[8]{0:T(128)S(1)} %copy-done.4, s32[2,32]{1,0:T(2,128)S(1)} %bitcast.3, f32[8,16,128]{2,1,0:T(8,128)S(1)} %copy-done.1, bf16[8,16,128,128]{3,2,1,0:T(8,128)(2,1)S(1)} %copy-done), custom_call_target="tpu_custom_call" | custom-call | tf_op jit(solution)/shard_map/pallas_call | solution.py:324
  76.9 0.7 copy.7
Async XLA Ops:
  0.0 2.2 %copy-start = (bf16[8,16,128,128]{3,2,1,0:T(8,128)(2,1)S(1)}, bf16[8,16,128,128]{3,2,1,0:T(8,128)(2,1)}, u32[]{:S(2)}) copy-start(bf16[8,16,128,128]{3,2,1,0:T(8,128)(2,1)} %tiles_hbm.1) | copy-start | bytes 12582916
  2.2 0.8 %copy-start.1 = (f32[8,16,128]{2,1,0:T(8,128)S(1)}, f32[8,16,128]{2,1,0:T(8,128)}, u32[]{:S(2)}) copy-start(f32[8,16,128]{2,1,0:T(8,128)} %basis.1) | copy-start | bytes 196612
  3.0 0.7 copy-start.2
  3.7 0.7 copy-start.3
  4.4 0.7 copy-start.4

commit v2 on v1

--- a/solution.py
+++ b/solution.py
@@ -11,6 +11,8 @@
 RIM = 2
 ITERS = 3
 MINLIVE = 10
+PIECES = 3
+UNROLL = 4
 MESH = pl.DeviceIdType.MESH
 F32 = jnp.float32
 BF16 = jnp.bfloat16
@@ -18,20 +20,36 @@
 NT = (((1,), (1,)), ((), ()))
 
 
-def split(x):
-    high = x.astype(BF16)
-    return high, (x - high.astype(F32)).astype(BF16)
+def split(x, count):
+    parts = []
+    for _ in range(count):
+        parts.append(x.astype(BF16))
+        x = x - parts[-1].astype(F32)
+    return parts
+
+
+def send_order(peers):
+    far = [(2, 2), (1, 2), (2, 1), (3, 2), (2, 3), (1, 1), (3, 3), (1, 3), (3, 1)]
+    near = [(2, 0), (0, 2), (1, 0), (0, 1), (3, 0), (0, 3)]
+    order = [(y, x, c) for y, x in far + near for c in (0, 1)] + [(0, 0, 1)]
+    if peers != 32:
+        order = [(0, 0, step) for step in range(1, peers)]
+    return order
 
 
 def kernel(
     groups,
     peers,
+    cols_hbm,
+    count_hbm,
+    wanted_hbm,
+    basis_hbm,
+    tiles_hbm,
+    out,
     cols,
     count,
     wanted,
     basis,
-    tiles_hbm,
-    out,
     tiles,
     inv_root,
     applied,
@@ -53,7 +71,6 @@
     gram_far_1,
     gram_far_2,
     tile_sem,
-    table_sem,
     list_sem,
     send_sem,
     recv_sem,
@@ -63,6 +80,7 @@
     near_recv,
     far_send,
     far_recv,
+    arg_sem,
 ):
     blocks, vectors, side = basis.shape
     per_row = cols.shape[1]
@@ -79,12 +97,32 @@
     def peer(step):
         return lax.rem(me + step, peers)
 
+    def offset_peer(offset):
+        dy, dx, dc = offset
+        if peers != 32:
+            return peer(dc)
+        y, x, c = me // 8, lax.rem(me // 2, 4), lax.rem(me, 2)
+        return lax.rem(y + dy, 4) * 8 + lax.rem(x + dx, 4) * 2 + lax.rem(c + dc, 2)
+
     def far_peer(step):
         return lax.rem(group + step, groups)
 
     def copy_in(b):
         return pltpu.make_async_copy(tiles_hbm.at[b], tiles.at[b], tile_sem.at[b])
 
+    arguments = [
+        pltpu.make_async_copy(source, target, arg_sem.at[i])
+        for i, (source, target) in enumerate(
+            (
+                (wanted_hbm, wanted),
+                (count_hbm, count),
+                (basis_hbm, basis),
+                (cols_hbm, cols),
+            )
+        )
+    ]
+    for copy in arguments:
+        copy.start()
     for b in range(blocks):
         copy_in(b).start()
 
@@ -98,6 +136,8 @@
     def _(step):
         pl.semaphore_signal(barrier, inc=1, device_id=(far_peer(step), me), device_id_type=MESH)
 
+    for copy in arguments:
+        copy.wait()
     pl.semaphore_wait(barrier, peers - 1 + groups - 1)
 
     @pl.loop(1, peers)
@@ -111,7 +151,7 @@
             device_id_type=MESH,
         ).start()
 
-    ones = jnp.ones((vectors, 2 * side), BF16)
+    ones = jnp.ones((vectors, 3 * side), BF16)
 
     @pl.loop(0, blocks)
     def _(b):
@@ -125,7 +165,7 @@
                 square = square * jnp.where(s < live, 1.0, 0.0).astype(F32)
             total = total + square
         sums = lax.dot_general(
-            ones, jnp.concatenate(split(total), axis=1), NT, preferred_element_type=F32
+            ones, jnp.concatenate(split(total, 3), axis=1), NT, preferred_element_type=F32
         )
         root = 1.0 / jnp.sqrt(jnp.sqrt(1e-06 + sums))
         inv_root[b] = root
@@ -137,7 +177,7 @@
     part = table.at[pl.ds(0, peers - 1)]
     list_wait(part, list_sem.at[0]).wait()
     list_wait(part, list_sem.at[1]).wait()
-    to_scalar = pltpu.make_async_copy(table, table_s, table_sem)
+    to_scalar = pltpu.make_async_copy(table, table_s, arg_sem.at[0])
     to_scalar.start()
     to_scalar.wait()
 
@@ -155,9 +195,8 @@
                 device_id_type=MESH,
             ).start()
 
-        @pl.loop(1, peers)
-        def _(step):
-            q = peer(step)
+        for offset in send_order(peers):
+            q = offset_peer(offset)
             for c in range(SLOTS):
                 pick = jnp.clip(table_s[q, c, me] - first_block, 0, blocks - 1)
                 stage[t, q, c] = source[pick]
@@ -177,9 +216,8 @@
             list_wait(rim.at[t, at], rim_recv.at[t, at]).wait()
 
     def put_pieces(at, value):
-        high, low = split(value)
-        pieces[pl.ds(at, value.shape[0]), 0:vectors] = high
-        pieces[pl.ds(at, value.shape[0]), vectors : 2 * vectors] = low
+        for i, part in enumerate(split(value, PIECES)):
+            pieces[pl.ds(at, value.shape[0]), i * vectors : (i + 1) * vectors] = part
 
     def multiply(t):
         put_pieces(0, own[t][...])
@@ -191,7 +229,7 @@
         for at in range(2):
             put_pieces(blocks + SLOTS * peers + RIM * at, rim[t, at])
 
-        @pl.loop(0, blocks)
+        @pl.loop(0, blocks, unroll=UNROLL)
         def _(b):
             live = count[b]
             picked = []
@@ -206,7 +244,10 @@
                 NT,
                 preferred_element_type=F32,
             )
-            applied[b] = (both[:vectors] + both[vectors:]) * inv_root[b]
+            product = both[:vectors]
+            for i in range(1, PIECES):
+                product = product + both[i * vectors : (i + 1) * vectors]
+            applied[b] = product * inv_root[b]
 
     def wide(ref):
         return jnp.concatenate([ref[b] for b in range(blocks)], axis=1)
@@ -260,15 +301,23 @@
         full = jnp.where(own_lane, rows, 0.0)
         for shift in (64, 32, 16):
             full = full + pltpu.roll(full, shift, 1)
-        both = jnp.where(lane_of < vectors, jnp.where(lane_of == row_of, 1.0, 0.0), full)
+        columns = [
+            jnp.broadcast_to(full[:, k : k + 1], (vectors, side)) for k in range(vectors)
+        ]
+        inverse = jnp.where(lane_of == row_of, 1.0, 0.0).astype(F32)
         pivots = jnp.zeros((vectors, side), F32)
+
+        def row(value, j):
+            return jnp.broadcast_to(value[j : j + 1], (vectors, side))
+
         for j in range(vectors):
-            pivot_row = jnp.broadcast_to(both[j : j + 1], (vectors, side))
-            column = jnp.broadcast_to(both[:, vectors + j : vectors + j + 1], (vectors, side))
-            pivot = jnp.broadcast_to(pivot_row[:, vectors + j : vectors + j + 1], (vectors, side))
+            pivot = row(columns[j], j)
             pivots = jnp.where(row_of == j, pivot, pivots)
-            both = jnp.where(row_of > j, both - (column / pivot) * pivot_row, both)
-        return (both / jnp.sqrt(pivots))[:, :vectors]
+            factor = jnp.where(row_of > j, columns[j] / pivot, 0.0)
+            inverse = inverse - factor * row(inverse, j)
+            for k in range(j + 1, vectors):
+                columns[k] = columns[k] - factor * row(columns[k], j)
+        return (inverse / jnp.sqrt(pivots))[:, :vectors]
 
     def normalise(inverse, value):
         return lax.dot_general(
@@ -283,25 +332,35 @@
         for b in range(blocks):
             out[t, b] = value[:, b * side : (b + 1) * side]
 
-    pieces[zero_slot] = jnp.zeros((2 * vectors, side), BF16)
+    pieces[zero_slot] = jnp.zeros((PIECES * vectors, side), BF16)
+    def spread(value, target):
+        for b in range(blocks):
+            target[b] = value[:, b * side : (b + 1) * side] * inv_root[b]
+
     send(0)
     wait_recv(0)
     multiply(0)
-    current = wide(applied)
-    for t in range(ITERS):
-        if t + 1 < ITERS:
-            for b in range(blocks):
-                own[t + 1][b] = current[:, b * side : (b + 1) * side] * inv_root[b]
-        gram_start(t, current)
-        if t + 1 < ITERS:
-            send(t + 1)
-        gram_far_start(t)
-        inverse = gram_end(t)
-        store_out(t, normalise(inverse, current))
-        if t + 1 < ITERS:
-            wait_recv(t + 1)
-            multiply(t + 1)
-            current = normalise(inverse, wide(applied))
+    first = wide(applied)
+    spread(first, own_1)
+    gram_start(0, first)
+    send(1)
+    gram_far_start(0)
+    wait_recv(1)
+    multiply(1)
+    second = wide(applied)
+    spread(second, own_2)
+    gram_start(1, second)
+    send(2)
+    store_out(0, normalise(gram_end(0), first))
+    gram_far_start(1)
+    wait_recv(2)
+    multiply(2)
+    inverse = gram_end(1)
+    third = normalise(inverse, wide(applied))
+    gram_start(2, third)
+    store_out(1, normalise(inverse, second))
+    gram_far_start(2)
+    store_out(2, normalise(gram_end(2), third))
 
     for t in range(ITERS):
         list_wait(stage.at[t, pl.ds(0, peers - 1)], send_sem.at[t]).wait()
@@ -318,21 +377,18 @@
     slots = blocks + SLOTS * peers + 2 * RIM + 1
     dma = pltpu.SemaphoreType.DMA
     vmem = pltpu.VMEM
-    smem = pl.BlockSpec(memory_space=pltpu.SMEM)
     near = vmem((peers, vectors // 8, side), F32)
     far = vmem((groups, vectors // 8, side), F32)
     return pl.pallas_call(
         functools.partial(kernel, groups, peers),
         out_shape=jax.ShapeDtypeStruct((ITERS, blocks, vectors, side), F32),
-        in_specs=[
-            smem,
-            smem,
-            pl.BlockSpec(memory_space=pltpu.VMEM),
-            pl.BlockSpec(memory_space=pltpu.VMEM),
-            pl.BlockSpec(memory_space=pl.ANY),
-        ],
+        in_specs=[pl.BlockSpec(memory_space=pltpu.HBM)] * 5,
         out_specs=pl.BlockSpec(memory_space=pltpu.VMEM),
         scratch_shapes=[
+            pltpu.SMEM(tile_cols.shape, jnp.int32),
+            pltpu.SMEM(tile_count.shape, jnp.int32),
+            vmem(wanted.shape, jnp.int32),
+            vmem((blocks, vectors, side), F32),
             vmem((blocks, per_row, side, side), BF16),
             vmem((blocks, vectors, side), F32),
             vmem((blocks, vectors, side), F32),
@@ -342,7 +398,7 @@
         + [vmem((peers, SLOTS, vectors, side), F32)] * ITERS
         + [
             vmem((ITERS, 2, RIM, vectors, side), F32),
-            vmem((slots, 2 * vectors, side), BF16),
+            vmem((slots, PIECES * vectors, side), BF16),
             vmem((peers, SLOTS, peers), jnp.int32),
             pltpu.SMEM((peers, SLOTS, peers), jnp.int32),
         ]
@@ -350,7 +406,6 @@
         + [far] * ITERS
         + [
             dma((blocks,)),
-            dma,
             dma((2,)),
             dma((ITERS,)),
             dma((ITERS,)),
@@ -360,9 +415,10 @@
             dma((ITERS,)),
             dma((ITERS,)),
             dma((ITERS,)),
+            dma((4,)),
         ],
         compiler_params=pltpu.CompilerParams(
-            collective_id=0, has_side_effects=True, vmem_limit_bytes=40 << 20
+            collective_id=0, has_side_effects=True, vmem_limit_bytes=60 << 20
         ),
     )(tile_cols, tile_count, wanted, start_basis, tiles)
 

time: 77.8 us -> 63.6 us (0.82)
  Pallas kernels: 71.9 us -> 61.8 us
  local copies, waits for them, and re-layouts: 5.73 us -> 1.62 us
    pallas_call x1, Pallas kernels: 71.9 us -> 61.8 us  [local(): pl.pallas_call(functools.partial(kernel, groups, peers), out_shape=jax.Sh...]
    unnamed x11 -> x1, local copies, waits for them, and re-layouts: 5.73 us -> 1.62 us
where the time goes in v2:
time: 63.6 us; the launch traced here: 63.5 us
  Pallas kernels  61.8 us (97%)
  local copies, waits for them, and re-layouts  1.62 us (3%)
    pallas_call x1, Pallas kernels, local(): pl.pallas_call(functools.partial(kernel, groups, peers), out_shape=jax.Sh...  61.8 us
    unnamed x1, local copies, waits for them, and re-layouts  1.62 us

profile of v2, /device:TPU:1, one launch (start us, length us, event | category | flops | bytes accessed | tf_op | source)
XLA Modules:
  0.0 63.5 jit_solution(4752548422309084805)
XLA Ops:
  0.0 61.8 %shard_map.55 = f32[3,8,16,128]{3,2,1,0:T(8,128)} custom-call(s32[8,16]{1,0:T(8,128)} %cols_hbm.1, s32[8]{0:T(128)} %count_hbm.1, s32[2,32]{1,0:T(2,128)} %bitcast.3, f32[8,16,128]{2,1,0:T(8,128)} %basis_hbm.1, bf16[8,16,128,128]{3,2,1,0:T(8,128)(2,1)} %tiles_hbm.1), custom_call_target="tpu_custom_call" | custom-call | tf_op jit(solution)/shard_map/pallas_call | solution.py:382
  61.9 1.6 %copy.7 = f32[3,8,16,128]{3,2,1,0:T(8,128)} copy(f32[3,8,16,128]{3,2,1,0:T(8,128)} %shard_map.55) | data formatting | bytes 393216

commit v3 on v2

v3 whole, which is shorter than its diff:
```python
import functools

import jax
import jax.numpy as jnp
from jax import lax
from jax.experimental import pallas as pl
from jax.experimental.pallas import tpu as pltpu
from jax.sharding import PartitionSpec as P

SLOTS = 2
RIM = 2
ITERS = 3
MINLIVE = 10
HALVES = 2
UNROLL = 8
UNROLL_PIECES = 8
MESH = pl.DeviceIdType.MESH
F32 = jnp.float32
BF16 = jnp.bfloat16
HIGHEST = lax.Precision.HIGHEST
NT = (((1,), (1,)), ((), ()))


def split(x, count):
    parts = []
    for _ in range(count):
        parts.append(x.astype(BF16))
        x = x - parts[-1].astype(F32)
    return parts


def send_order(peers):
    far = [(2, 2), (1, 2), (2, 1), (3, 2), (2, 3), (1, 1), (3, 3), (1, 3), (3, 1)]
    near = [(2, 0), (0, 2), (1, 0), (0, 1), (3, 0), (0, 3)]
    order = [(y, x, c) for y, x in far + near for c in (0, 1)] + [(0, 0, 1)]
    if peers != 32:
        order = [(0, 0, step) for step in range(1, peers)]
    return order


def kernel(
    groups,
    peers,
    cols_hbm,
    count_hbm,
    wanted_hbm,
    basis_hbm,
    tiles_hbm,
    out_hbm,
    cols,
    count,
    wanted,
    basis,
    tiles,
    inv_root,
    applied,
    out,
    own,
    stage,
    recv,
    rim,
    pieces,
    table,
    table_s,
    gram_near,
    gram_far,
    arg_sem,
    tile_sem,
    list_sem,
    send_sem,
    recv_sem,
    rim_send,
    rim_recv,
    near_sem,
    far_sem,
    out_sem,
):
    blocks, vectors, side = basis.shape
    half = vectors // HALVES
    per_row = cols.shape[1]
    group = lax.axis_index("group")
    me = lax.axis_index("row")
    up = lax.rem(group + 1, groups)
    down = lax.rem(group + groups - 1, groups)
    zero_slot = blocks + SLOTS * peers + 2 * RIM

    def peer(step):
        return lax.rem(me + step, peers)

    def offset_peer(offset):
        dy, dx, dc = offset
        if peers != 32:
            return peer(dc)
        y, x, c = me // 8, lax.rem(me // 2, 4), lax.rem(me, 2)
        return lax.rem(y + dy, 4) * 8 + lax.rem(x + dx, 4) * 2 + lax.rem(c + dc, 2)

    def far_peer(step):
        return lax.rem(group + step, groups)

    def remote(source, target, sems, group_to, row_to):
        return pltpu.make_async_remote_copy(
            src_ref=source,
            dst_ref=target,
            send_sem=sems[0],
            recv_sem=sems[1],
            device_id=(group_to, row_to),
            device_id_type=MESH,
        )

    def wait_for(ref, sem):
        pltpu.make_async_copy(ref, ref, sem).wait()

    def copy_in(b):
        return pltpu.make_async_copy(tiles_hbm.at[b], tiles.at[b], tile_sem.at[b])

    arguments = [
        pltpu.make_async_copy(source, target, arg_sem.at[i])
        for i, (source, target) in enumerate(
            (
                (wanted_hbm, wanted),
                (count_hbm, count),
                (basis_hbm, basis),
                (cols_hbm, cols),
            )
        )
    ]

    barrier = pltpu.get_barrier_semaphore()

    @pl.loop(1, peers)
    def _(step):
        pl.semaphore_signal(barrier, inc=1, device_id=(group, peer(step)), device_id_type=MESH)

    @pl.loop(1, groups)
    def _(step):
        pl.semaphore_signal(barrier, inc=1, device_id=(far_peer(step), me), device_id_type=MESH)

    for copy in arguments:
        copy.start()
    for b in range(blocks):
        copy_in(b).start()
    for copy in arguments:
        copy.wait()
    pl.semaphore_wait(barrier, peers - 1 + groups - 1)

    for offset in send_order(peers):
        remote(
            wanted, table.at[me], (list_sem.at[0], list_sem.at[1]), group, offset_peer(offset)
        ).start()

    ones = jnp.ones((vectors, 3 * side), BF16)

    @pl.loop(0, blocks)
    def _(b):
        copy_in(b).wait()
        live = count[b]
        total = jnp.zeros((side, side), F32)
        for s in range(per_row):
            wide = tiles[b, s].astype(F32)
            square = wide * wide
            if s >= MINLIVE:
                square = square * jnp.where(s < live, 1.0, 0.0).astype(F32)
            total = total + square
        sums = lax.dot_general(
            ones, jnp.concatenate(split(total, 3), axis=1), NT, preferred_element_type=F32
        )
        root = 1.0 / jnp.sqrt(jnp.sqrt(1e-06 + sums))
        inv_root[b] = root
        value = basis[b] * root
        for h in range(HALVES):
            own[0, h, b] = value[h * half : (h + 1) * half]

    pieces[zero_slot] = jnp.zeros(pieces.shape[1:], BF16)
    part = table.at[pl.ds(0, peers - 1)]
    wait_for(part, list_sem.at[0])
    wait_for(part, list_sem.at[1])
    to_scalar = pltpu.make_async_copy(table, table_s, arg_sem.at[0])
    to_scalar.start()
    to_scalar.wait()

    first_block = (group * peers + me) * blocks

    def send(t, h):
        for at, (lo, target) in enumerate(((blocks - RIM, up), (0, down))):
            remote(
                own.at[t, h, pl.ds(lo, RIM)],
                rim.at[t, h, at],
                (rim_send.at[t, h, at], rim_recv.at[t, h, at]),
                target,
                me,
            ).start()
        for offset in send_order(peers):
            q = offset_peer(offset)
            for c in range(SLOTS):
                pick = jnp.clip(table_s[q, c, me] - first_block, 0, blocks - 1)
                stage[t, h, q, c] = own[t, h, pick]
            remote(
                stage.at[t, h, q],
                recv.at[t, h, me],
                (send_sem.at[t, h], recv_sem.at[t, h]),
                group,
                q,
            ).start()

    def put_pieces(at, value):
        high = value.astype(BF16).astype(F32)
        rest = value - high
        middle = rest.astype(BF16).astype(F32)
        parts = [high, middle, rest - middle, jnp.zeros_like(value)]
        pieces[pl.ds(at, value.shape[0])] = jnp.concatenate(parts, axis=1).astype(BF16)

    def multiply(t, h):
        put_pieces(0, own[t, h])
        wait_for(recv.at[t, h, pl.ds(0, peers - 1)], recv_sem.at[t, h])

        @pl.loop(0, peers, unroll=UNROLL_PIECES)
        def _(q):
            put_pieces(blocks + SLOTS * q, recv[t, h, q])

        for at in range(2):
            wait_for(rim.at[t, h, at], rim_recv.at[t, h, at])
            put_pieces(blocks + SLOTS * peers + RIM * at, rim[t, h, at])

        @pl.loop(0, blocks, unroll=UNROLL)
        def _(b):
            live = count[b]
            picked = []
            for s in range(per_row):
                slot = cols[b, s]
                if s >= MINLIVE:
                    slot = jnp.where(s < live, slot, zero_slot)
                picked.append(pieces[slot])
            both = lax.dot_general(
                jnp.concatenate(picked, axis=1),
                jnp.concatenate([tiles[b, s] for s in range(per_row)], axis=1),
                NT,
                preferred_element_type=F32,
            )
            product = both[:half] + both[half : 2 * half] + both[2 * half : 3 * half]
            root = inv_root[b, :half]
            product = product * root
            applied[t, h, b] = product
            own[t + 1, h, b] = product * root

    def wide(ref):
        return jnp.concatenate(
            [
                jnp.concatenate([ref[h, b] for b in range(blocks)], axis=1)
                for h in range(HALVES)
            ],
            axis=0,
        )

    row_of = lax.broadcasted_iota(jnp.int32, (vectors, side), 0)
    lane_of = lax.broadcasted_iota(jnp.int32, (vectors, side), 1)
    own_lane = lax.rem(row_of, 8) == lane_of // vectors
    row_total = groups * peers * blocks * side

    def gram_start(t, value):
        gram = lax.dot_general(
            value,
            jnp.concatenate([value] * (side // vectors), axis=0),
            NT,
            precision=HIGHEST,
            preferred_element_type=F32,
        )
        packed = jnp.sum(jnp.where(own_lane, gram, 0.0).reshape(vectors // 8, 8, side), axis=1)
        gram_near[t, me] = packed

        @pl.loop(1, peers)
        def _(step):
            here = gram_near.at[t, me]
            remote(here, here, (near_sem.at[t, 0], near_sem.at[t, 1]), group, peer(step)).start()

    def gram_far_start(t):
        wait_for(gram_near.at[t, pl.ds(0, peers - 1)], near_sem.at[t, 1])
        gram_far[t, group] = jnp.sum(gram_near[t], axis=0)

        @pl.loop(1, groups)
        def _(step):
            here = gram_far.at[t, group]
            remote(here, here, (far_sem.at[t, 0], far_sem.at[t, 1]), far_peer(step), me).start()

    def gram_end(t):
        wait_for(gram_far.at[t, pl.ds(0, groups - 1)], far_sem.at[t, 1])
        packed = jnp.sum(gram_far[t], axis=0) / row_total
        rows = jnp.broadcast_to(packed[:, None, :], (vectors // 8, 8, side)).reshape(vectors, side)
        full = jnp.where(own_lane, rows, 0.0)
        for shift in (64, 32, 16):
            full = full + pltpu.roll(full, shift, 1)
        columns = [
            jnp.broadcast_to(full[:, k : k + 1], (vectors, side)) for k in range(vectors)
        ]
        inverse = jnp.where(lane_of == row_of, 1.0, 0.0).astype(F32)
        pivots = jnp.zeros((vectors, side), F32)

        def row(value, j):
            return jnp.broadcast_to(value[j : j + 1], (vectors, side))

        for j in range(vectors):
            pivot = row(columns[j], j)
            pivots = jnp.where(row_of == j, pivot, pivots)
            factor = jnp.where(row_of > j, columns[j] / pivot, 0.0)
            inverse = inverse - factor * row(inverse, j)
            for k in range(j + 1, vectors):
                columns[k] = columns[k] - factor * row(columns[k], j)
        return (inverse / jnp.sqrt(pivots))[:, :vectors]

    def normalise(inverse, value):
        return lax.dot_general(
            inverse,
            value,
            (((1,), (0,)), ((), ())),
            precision=HIGHEST,
            preferred_element_type=F32,
        )

    def copy_out(t):
        return pltpu.make_async_copy(out.at[t], out_hbm.at[t], out_sem.at[t])

    def store_out(t, value):
        for b in range(blocks):
            out[t, b] = value[:, b * side : (b + 1) * side]
        copy_out(t).start()

    @pl.loop(0, HALVES)
    def _(h):
        send(0, h)

    last = HALVES - 1

    @pl.loop(0, ITERS)
    def _(t):
        @pl.loop(0, HALVES)
        def _(h):
            @pl.when((t == 2) & (h == 0))
            def _():
                gram_far_start(1)

            multiply(t, h)

            @pl.when((t < ITERS - 1) & (h == last))
            def _():
                gram_start(t, wide(applied.at[t]))

            @pl.when(t < ITERS - 1)
            def _():
                send(t + 1, h)

            @pl.when((t == 1) & (h == 0))
            def _():
                gram_far_start(0)

            @pl.when((t == 1) & (h == last))
            def _():
                store_out(0, normalise(gram_end(0), wide(applied.at[0])))

    inverse = gram_end(1)
    third = normalise(inverse, wide(applied.at[2]))
    gram_start(2, third)
    store_out(1, normalise(inverse, wide(applied.at[1])))
    gram_far_start(2)
    store_out(2, normalise(gram_end(2), third))

    @pl.loop(0, ITERS)
    def _(t):
        for h in range(HALVES):
            wait_for(stage.at[t, h, pl.ds(0, peers - 1)], send_sem.at[t, h])
            for at in range(2):
                wait_for(rim.at[t, h, at], rim_send.at[t, h, at])
        wait_for(gram_near.at[t, pl.ds(0, peers - 1)], near_sem.at[t, 0])
        wait_for(gram_far.at[t, pl.ds(0, groups - 1)], far_sem.at[t, 0])

    for t in range(ITERS):
        copy_out(t).wait()


def local(groups, peers, start_basis, tiles, tile_cols, tile_count, recv_list):
    blocks, per_row, side, _ = tiles.shape
    vectors = start_basis.shape[1]
    half = vectors // HALVES
    wanted = jnp.transpose(recv_list.reshape(peers, SLOTS))
    slots = blocks + SLOTS * peers + 2 * RIM + 1
    dma = pltpu.SemaphoreType.DMA
    vmem = pltpu.VMEM
    out_shape = (ITERS, blocks, vectors, side)
    return pl.pallas_call(
        functools.partial(kernel, groups, peers),
        out_shape=jax.ShapeDtypeStruct(out_shape, F32),
        in_specs=[pl.BlockSpec(memory_space=pltpu.HBM)] * 5,
        out_specs=pl.BlockSpec(memory_space=pltpu.HBM),
        scratch_shapes=[
            pltpu.SMEM(tile_cols.shape, jnp.int32),
            pltpu.SMEM(tile_count.shape, jnp.int32),
            vmem(wanted.shape, jnp.int32),
            vmem((blocks, vectors, side), F32),
            vmem((blocks, per_row, side, side), BF16),
            vmem((blocks, vectors, side), F32),
            vmem((ITERS, HALVES, blocks, half, side), F32),
            vmem(out_shape, F32),
            vmem((ITERS + 1, HALVES, blocks, half, side), F32),
            vmem((ITERS, HALVES, peers, SLOTS, half, side), F32),
            vmem((ITERS, HALVES, peers, SLOTS, half, side), F32),
            vmem((ITERS, HALVES, 2, RIM, half, side), F32),
            vmem((slots, 4 * half, side), BF16),
            vmem((peers, SLOTS, peers), jnp.int32),
            pltpu.SMEM((peers, SLOTS, peers), jnp.int32),
            vmem((ITERS, peers, vectors // 8, side), F32),
            vmem((ITERS, groups, vectors // 8, side), F32),
            dma((4,)),
            dma((blocks,)),
            dma((2,)),
            dma((ITERS, HALVES)),
            dma((ITERS, HALVES)),
            dma((ITERS, HALVES, 2)),
            dma((ITERS, HALVES, 2)),
            dma((ITERS, 2)),
            dma((ITERS, 2)),
            dma((ITERS,)),
        ],
        compiler_params=pltpu.CompilerParams(
            collective_id=0, has_side_effects=True, vmem_limit_bytes=60 << 20
        ),
    )(tile_cols, tile_count, wanted, start_basis, tiles)


def solution(mesh):
    placed = (
        P(("group", "row"), None, None),
        P(("group", "row"), None, None, None),
        P(("group", "row"), None),
        P(("group", "row")),
        P("group", "row", None, None),
    )
    return jax.shard_map(
        functools.partial(local, mesh.shape["group"], mesh.shape["row"]),
        mesh=mesh,
        in_specs=placed,
        out_specs=P(None, ("group", "row"), None, None),
        check_vma=False,
    )
```

time: 63.6 us -> 58.8 us (0.925)
  Pallas kernels: 61.8 us -> 57.1 us
    pallas_call x1, Pallas kernels: 61.8 us -> 57.1 us  [local(): pl.pallas_call(functools.partial(kernel, groups, peers), out_shape=jax.Sh...]
where the time goes in v3:
time: 58.8 us; the launch traced here: 58.7 us
  Pallas kernels  57.1 us (97%)
  local copies, waits for them, and re-layouts  1.62 us (3%)
    pallas_call x1, Pallas kernels, local(): pl.pallas_call(functools.partial(kernel, groups, peers), out_shape=jax.Sh...  57.1 us
    unnamed x1, local copies, waits for them, and re-layouts  1.62 us

profile of v3, /device:TPU:1, one launch (start us, length us, event | category | flops | bytes accessed | tf_op | source)
XLA Modules:
  0.0 58.7 jit_solution(89533106573059135)
XLA Ops:
  0.0 57.1 %shard_map.55 = f32[3,8,16,128]{3,2,1,0:T(8,128)} custom-call(s32[8,16]{1,0:T(8,128)} %cols_hbm.1, s32[8]{0:T(128)} %count_hbm.1, s32[2,32]{1,0:T(2,128)} %bitcast.3, f32[8,16,128]{2,1,0:T(8,128)} %basis_hbm.1, bf16[8,16,128,128]{3,2,1,0:T(8,128)(2,1)} %tiles_hbm.1), custom_call_target="tpu_custom_call" | custom-call | tf_op jit(solution)/shard_map/pallas_call | solution.py:387
  57.1 1.6 %copy.7 = f32[3,8,16,128]{3,2,1,0:T(8,128)} copy(f32[3,8,16,128]{3,2,1,0:T(8,128)} %shard_map.55) | data formatting | bytes 393216

commit v4 on v3

--- a/solution.py
+++ b/solution.py
@@ -21,14 +21,6 @@
 NT = (((1,), (1,)), ((), ()))
 
 
-def split(x, count):
-    parts = []
-    for _ in range(count):
-        parts.append(x.astype(BF16))
-        x = x - parts[-1].astype(F32)
-    return parts
-
-
 def send_order(peers):
     far = [(2, 2), (1, 2), (2, 1), (3, 2), (2, 3), (1, 1), (3, 3), (1, 3), (3, 1)]
     near = [(2, 0), (0, 2), (1, 0), (0, 1), (3, 0), (0, 3)]
@@ -46,15 +38,15 @@
     wanted_hbm,
     basis_hbm,
     tiles_hbm,
-    out_hbm,
+    out,
     cols,
     count,
     wanted,
     basis,
+    tiles_in,
     tiles,
     inv_root,
     applied,
-    out,
     own,
     stage,
     recv,
@@ -73,7 +65,6 @@
     rim_recv,
     near_sem,
     far_sem,
-    out_sem,
 ):
     blocks, vectors, side = basis.shape
     half = vectors // HALVES
@@ -111,7 +102,7 @@
         pltpu.make_async_copy(ref, ref, sem).wait()
 
     def copy_in(b):
-        return pltpu.make_async_copy(tiles_hbm.at[b], tiles.at[b], tile_sem.at[b])
+        return pltpu.make_async_copy(tiles_hbm.at[b], tiles_in.at[b], tile_sem.at[b])
 
     arguments = [
         pltpu.make_async_copy(source, target, arg_sem.at[i])
@@ -148,22 +139,19 @@
             wanted, table.at[me], (list_sem.at[0], list_sem.at[1]), group, offset_peer(offset)
         ).start()
 
-    ones = jnp.ones((vectors, 3 * side), BF16)
-
     @pl.loop(0, blocks)
     def _(b):
         copy_in(b).wait()
         live = count[b]
         total = jnp.zeros((side, side), F32)
         for s in range(per_row):
-            wide = tiles[b, s].astype(F32)
-            square = wide * wide
+            turned = tiles_in[b, s].astype(F32).T
+            tiles[b, s * side : (s + 1) * side] = turned.astype(BF16)
+            square = turned * turned
             if s >= MINLIVE:
                 square = square * jnp.where(s < live, 1.0, 0.0).astype(F32)
             total = total + square
-        sums = lax.dot_general(
-            ones, jnp.concatenate(split(total, 3), axis=1), NT, preferred_element_type=F32
-        )
+        sums = jnp.broadcast_to(jnp.sum(total, axis=0, keepdims=True), (vectors, side))
         root = 1.0 / jnp.sqrt(jnp.sqrt(1e-06 + sums))
         inv_root[b] = root
         value = basis[b] * root
@@ -232,8 +220,8 @@
                 picked.append(pieces[slot])
             both = lax.dot_general(
                 jnp.concatenate(picked, axis=1),
-                jnp.concatenate([tiles[b, s] for s in range(per_row)], axis=1),
-                NT,
+                tiles[b],
+                (((1,), (0,)), ((), ())),
                 preferred_element_type=F32,
             )
             product = both[:half] + both[half : 2 * half] + both[2 * half : 3 * half]
@@ -315,13 +303,9 @@
             preferred_element_type=F32,
         )
 
-    def copy_out(t):
-        return pltpu.make_async_copy(out.at[t], out_hbm.at[t], out_sem.at[t])
-
     def store_out(t, value):
         for b in range(blocks):
             out[t, b] = value[:, b * side : (b + 1) * side]
-        copy_out(t).start()
 
     @pl.loop(0, HALVES)
     def _(h):
@@ -370,9 +354,6 @@
                 wait_for(rim.at[t, h, at], rim_send.at[t, h, at])
         wait_for(gram_near.at[t, pl.ds(0, peers - 1)], near_sem.at[t, 0])
         wait_for(gram_far.at[t, pl.ds(0, groups - 1)], far_sem.at[t, 0])
-
-    for t in range(ITERS):
-        copy_out(t).wait()
 
 
 def local(groups, peers, start_basis, tiles, tile_cols, tile_count, recv_list):
@@ -384,20 +365,21 @@
     dma = pltpu.SemaphoreType.DMA
     vmem = pltpu.VMEM
     out_shape = (ITERS, blocks, vectors, side)
+    operands = (tile_cols, tile_count, wanted, start_basis, tiles)
     return pl.pallas_call(
         functools.partial(kernel, groups, peers),
         out_shape=jax.ShapeDtypeStruct(out_shape, F32),
         in_specs=[pl.BlockSpec(memory_space=pltpu.HBM)] * 5,
-        out_specs=pl.BlockSpec(memory_space=pltpu.HBM),
+        out_specs=pl.BlockSpec(memory_space=pltpu.VMEM),
         scratch_shapes=[
             pltpu.SMEM(tile_cols.shape, jnp.int32),
             pltpu.SMEM(tile_count.shape, jnp.int32),
             vmem(wanted.shape, jnp.int32),
             vmem((blocks, vectors, side), F32),
             vmem((blocks, per_row, side, side), BF16),
+            vmem((blocks, per_row * side, side), BF16),
             vmem((blocks, vectors, side), F32),
             vmem((ITERS, HALVES, blocks, half, side), F32),
-            vmem(out_shape, F32),
             vmem((ITERS + 1, HALVES, blocks, half, side), F32),
             vmem((ITERS, HALVES, peers, SLOTS, half, side), F32),
             vmem((ITERS, HALVES, peers, SLOTS, half, side), F32),
@@ -416,12 +398,11 @@
             dma((ITERS, HALVES, 2)),
             dma((ITERS, 2)),
             dma((ITERS, 2)),
-            dma((ITERS,)),
         ],
         compiler_params=pltpu.CompilerParams(
-            collective_id=0, has_side_effects=True, vmem_limit_bytes=60 << 20
+            collective_id=0, has_side_effects=True, vmem_limit_bytes=32 << 20
         ),
-    )(tile_cols, tile_count, wanted, start_basis, tiles)
+    )(*[pltpu.with_memory_space_constraint(value, pltpu.HBM) for value in operands])
 
 
 def solution(mesh):

time: 58.8 us -> 55.8 us (0.949)
  Pallas kernels: 57.1 us -> 55.1 us
  local copies, waits for them, and re-layouts: 1.62 us -> 0.68 us
    pallas_call x1, Pallas kernels: 57.1 us -> 55.1 us  [local(): pl.pallas_call(functools.partial(kernel, groups, peers), out_shape=jax.Sh...]
    unnamed x1, local copies, waits for them, and re-layouts: 1.62 us -> 0.68 us
where the time goes in v4:
time: 55.8 us
  Pallas kernels  55.1 us (99%)
  local copies, waits for them, and re-layouts  0.68 us (1%)
    pallas_call x1, Pallas kernels, local(): pl.pallas_call(functools.partial(kernel, groups, peers), out_shape=jax.Sh...  55.1 us

profile of v4, /device:TPU:1, one launch (start us, length us, event | category | flops | bytes accessed | tf_op | source)
XLA Modules:
  0.0 55.8 jit_solution(5538288020941901830)
XLA Ops:
  0.0 55.1 %shard_map.55 = f32[3,8,16,128]{3,2,1,0:T(8,128)S(1)} custom-call(s32[8,16]{1,0:T(8,128)} %cols_hbm.1, s32[8]{0:T(128)} %count_hbm.1, s32[2,32]{1,0:T(2,128)} %bitcast.3, f32[8,16,128]{2,1,0:T(8,128)} %basis_hbm.1, bf16[8,16,128,128]{3,2,1,0:T(8,128)(2,1)} %tiles_hbm.1), custom_call_target="tpu_custom_call" | custom-call | tf_op jit(solution)/shard_map/pallas_call | solution.py:369
  55.1 0.7 %copy.7 = f32[3,8,16,128]{3,2,1,0:T(8,128)} copy(f32[3,8,16,128]{3,2,1,0:T(8,128)S(1)} %shard_map.55) | data formatting | bytes 393216

commit v5 on v4

--- a/solution.py
+++ b/solution.py
@@ -19,6 +19,14 @@
 BF16 = jnp.bfloat16
 HIGHEST = lax.Precision.HIGHEST
 NT = (((1,), (1,)), ((), ()))
+
+
+def split(x, count):
+    parts = []
+    for _ in range(count):
+        parts.append(x.astype(BF16))
+        x = x - parts[-1].astype(F32)
+    return parts
 
 
 def send_order(peers):
@@ -56,6 +64,7 @@
     table_s,
     gram_near,
     gram_far,
+    first_inverse,
     arg_sem,
     tile_sem,
     list_sem,
@@ -118,13 +127,11 @@
 
     barrier = pltpu.get_barrier_semaphore()
 
-    @pl.loop(1, peers)
-    def _(step):
-        pl.semaphore_signal(barrier, inc=1, device_id=(group, peer(step)), device_id_type=MESH)
-
-    @pl.loop(1, groups)
-    def _(step):
+    for step in sorted(range(1, groups), key=lambda step: -min(step, groups - step)):
         pl.semaphore_signal(barrier, inc=1, device_id=(far_peer(step), me), device_id_type=MESH)
+    for offset in send_order(peers):
+        q = offset_peer(offset)
+        pl.semaphore_signal(barrier, inc=1, device_id=(group, q), device_id_type=MESH)
 
     for copy in arguments:
         copy.start()
@@ -160,7 +167,6 @@
 
     pieces[zero_slot] = jnp.zeros(pieces.shape[1:], BF16)
     part = table.at[pl.ds(0, peers - 1)]
-    wait_for(part, list_sem.at[0])
     wait_for(part, list_sem.at[1])
     to_scalar = pltpu.make_async_copy(table, table_s, arg_sem.at[0])
     to_scalar.start()
@@ -245,33 +251,37 @@
     row_total = groups * peers * blocks * side
 
     def gram_start(t, value):
-        gram = lax.dot_general(
-            value,
-            jnp.concatenate([value] * (side // vectors), axis=0),
-            NT,
-            precision=HIGHEST,
-            preferred_element_type=F32,
-        )
+        parts = split(value, 3)
+        all_parts = jnp.concatenate(parts, axis=0)
+        products = jnp.zeros((3 * vectors, side), F32)
+        for part in reversed(parts):
+            products = products + lax.dot_general(
+                all_parts,
+                jnp.concatenate([part] * (side // vectors), axis=0),
+                NT,
+                preferred_element_type=F32,
+            )
+        gram = products[2 * vectors :] + products[vectors : 2 * vectors] + products[:vectors]
         packed = jnp.sum(jnp.where(own_lane, gram, 0.0).reshape(vectors // 8, 8, side), axis=1)
-        gram_near[t, me] = packed
-
-        @pl.loop(1, peers)
-        def _(step):
-            here = gram_near.at[t, me]
-            remote(here, here, (near_sem.at[t, 0], near_sem.at[t, 1]), group, peer(step)).start()
-
-    def gram_far_start(t):
-        wait_for(gram_near.at[t, pl.ds(0, peers - 1)], near_sem.at[t, 1])
-        gram_far[t, group] = jnp.sum(gram_near[t], axis=0)
+        gram_far[t, group] = packed
 
         @pl.loop(1, groups)
         def _(step):
             here = gram_far.at[t, group]
             remote(here, here, (far_sem.at[t, 0], far_sem.at[t, 1]), far_peer(step), me).start()
 
+    def gram_near_start(t):
+        wait_for(gram_far.at[t, pl.ds(0, groups - 1)], far_sem.at[t, 1])
+        gram_near[t, me] = jnp.sum(gram_far[t], axis=0)
+
+        for offset in send_order(peers):
+            here = gram_near.at[t, me]
+            sems = (near_sem.at[t, 0], near_sem.at[t, 1])
+            remote(here, here, sems, group, offset_peer(offset)).start()
+
     def gram_end(t):
-        wait_for(gram_far.at[t, pl.ds(0, groups - 1)], far_sem.at[t, 1])
-        packed = jnp.sum(gram_far[t], axis=0) / row_total
+        wait_for(gram_near.at[t, pl.ds(0, peers - 1)], near_sem.at[t, 1])
+        packed = jnp.sum(gram_near[t], axis=0) / row_total
         rows = jnp.broadcast_to(packed[:, None, :], (vectors // 8, 8, side)).reshape(vectors, side)
         full = jnp.where(own_lane, rows, 0.0)
         for shift in (64, 32, 16):
@@ -317,9 +327,14 @@
     def _(t):
         @pl.loop(0, HALVES)
         def _(h):
-            @pl.when((t == 2) & (h == 0))
+            @pl.when((t == 1) & (h == 0))
             def _():
-                gram_far_start(1)
+                gram_near_start(0)
+
+            @pl.when((t == 2) & (h == last))
+            def _():
+                gram_near_start(1)
+                first_inverse[...] = gram_end(0)
 
             multiply(t, h)
 
@@ -331,20 +346,14 @@
             def _():
                 send(t + 1, h)
 
-            @pl.when((t == 1) & (h == 0))
-            def _():
-                gram_far_start(0)
-
-            @pl.when((t == 1) & (h == last))
-            def _():
-                store_out(0, normalise(gram_end(0), wide(applied.at[0])))
-
-    inverse = gram_end(1)
-    third = normalise(inverse, wide(applied.at[2]))
+    third = normalise(first_inverse[...], wide(applied.at[2]))
     gram_start(2, third)
-    store_out(1, normalise(inverse, wide(applied.at[1])))
-    gram_far_start(2)
+    store_out(0, normalise(first_inverse[...], wide(applied.at[0])))
+    gram_near_start(2)
+    store_out(1, normalise(gram_end(1), wide(applied.at[1])))
     store_out(2, normalise(gram_end(2), third))
+
+    wait_for(part, list_sem.at[0])
 
     @pl.loop(0, ITERS)
     def _(t):
@@ -389,6 +398,7 @@
             pltpu.SMEM((peers, SLOTS, peers), jnp.int32),
             vmem((ITERS, peers, vectors // 8, side), F32),
             vmem((ITERS, groups, vectors // 8, side), F32),
+            vmem((vectors, vectors), F32),
             dma((4,)),
             dma((blocks,)),
             dma((2,)),

time: 55.8 us -> 52.5 us (0.941)
  Pallas kernels: 55.1 us -> 51.8 us
    pallas_call x1, Pallas kernels: 55.1 us -> 51.8 us  [local(): pl.pallas_call(functools.partial(kernel, groups, peers), out_shape=jax.Sh...]
where the time goes in v5:
time: 52.5 us; the launch traced here: 52.4 us
  Pallas kernels  51.8 us (99%)
  local copies, waits for them, and re-layouts  0.68 us (1%)
    pallas_call x1, Pallas kernels, local(): pl.pallas_call(functools.partial(kernel, groups, peers), out_shape=jax.Sh...  51.8 us

profile of v5, /device:TPU:1, one launch (start us, length us, event | category | flops | bytes accessed | tf_op | source)
XLA Modules:
  0.0 52.4 jit_solution(7111365653173453851)
XLA Ops:
  0.0 51.8 %shard_map.55 = f32[3,8,16,128]{3,2,1,0:T(8,128)S(1)} custom-call(s32[8,16]{1,0:T(8,128)} %cols_hbm.1, s32[8]{0:T(128)} %count_hbm.1, s32[2,32]{1,0:T(2,128)} %bitcast.3, f32[8,16,128]{2,1,0:T(8,128)} %basis_hbm.1, bf16[8,16,128,128]{3,2,1,0:T(8,128)(2,1)} %tiles_hbm.1), custom_call_target="tpu_custom_call" | custom-call | tf_op jit(solution)/shard_map/pallas_call | solution.py:378
  51.8 0.7 %copy.7 = f32[3,8,16,128]{3,2,1,0:T(8,128)} copy(f32[3,8,16,128]{3,2,1,0:T(8,128)S(1)} %shard_map.55) | data formatting | bytes 393216

commit v6 on v5

--- a/solution.py
+++ b/solution.py
@@ -32,7 +32,7 @@
 def send_order(peers):
     far = [(2, 2), (1, 2), (2, 1), (3, 2), (2, 3), (1, 1), (3, 3), (1, 3), (3, 1)]
     near = [(2, 0), (0, 2), (1, 0), (0, 1), (3, 0), (0, 3)]
-    order = [(y, x, c) for y, x in far + near for c in (0, 1)] + [(0, 0, 1)]
+    order = [(y, x, c) for c in (0, 1) for y, x in far + near] + [(0, 0, 1)]
     if peers != 32:
         order = [(0, 0, step) for step in range(1, peers)]
     return order

time: 52.5 us -> 52.2 us (level)
  no operation moved by 1% of the time
where the time goes in v6:
time: 52.2 us; the launch traced here: 52.1 us
  Pallas kernels  51.4 us (98%)
  local copies, waits for them, and re-layouts  0.68 us (1%)
    pallas_call x1, Pallas kernels, local(): pl.pallas_call(functools.partial(kernel, groups, peers), out_shape=jax.Sh...  51.4 us

profile of v6, /device:TPU:1, one launch (start us, length us, event | category | flops | bytes accessed | tf_op | source)
XLA Modules:
  0.0 52.1 jit_solution(4694457961965431910)
XLA Ops:
  0.0 51.4 %shard_map.55 = f32[3,8,16,128]{3,2,1,0:T(8,128)S(1)} custom-call(s32[8,16]{1,0:T(8,128)} %cols_hbm.1, s32[8]{0:T(128)} %count_hbm.1, s32[2,32]{1,0:T(2,128)} %bitcast.3, f32[8,16,128]{2,1,0:T(8,128)} %basis_hbm.1, bf16[8,16,128,128]{3,2,1,0:T(8,128)(2,1)} %tiles_hbm.1), custom_call_target="tpu_custom_call" | custom-call | tf_op jit(solution)/shard_map/pallas_call | solution.py:378
  51.4 0.7 %copy.7 = f32[3,8,16,128]{3,2,1,0:T(8,128)} copy(f32[3,8,16,128]{3,2,1,0:T(8,128)S(1)} %shard_map.55) | data formatting | bytes 393216

commit v7 on v6

--- a/solution.py
+++ b/solution.py
@@ -327,27 +327,27 @@
     def _(t):
         @pl.loop(0, HALVES)
         def _(h):
-            @pl.when((t == 1) & (h == 0))
+            @pl.when((t == 1) & (h == last))
             def _():
                 gram_near_start(0)
 
             @pl.when((t == 2) & (h == last))
             def _():
-                gram_near_start(1)
                 first_inverse[...] = gram_end(0)
 
             multiply(t, h)
+
+            @pl.when(t < ITERS - 1)
+            def _():
+                send(t + 1, h)
 
             @pl.when((t < ITERS - 1) & (h == last))
             def _():
                 gram_start(t, wide(applied.at[t]))
 
-            @pl.when(t < ITERS - 1)
-            def _():
-                send(t + 1, h)
-
     third = normalise(first_inverse[...], wide(applied.at[2]))
     gram_start(2, third)
+    gram_near_start(1)
     store_out(0, normalise(first_inverse[...], wide(applied.at[0])))
     gram_near_start(2)
     store_out(1, normalise(gram_end(1), wide(applied.at[1])))

time: 52.2 us -> 51.2 us (0.981)
  Pallas kernels: 51.4 us -> 50.4 us
    pallas_call x1, Pallas kernels: 51.4 us -> 50.4 us  [local(): pl.pallas_call(functools.partial(kernel, groups, peers), out_shape=jax.Sh...]
where the time goes in v7:
time: 51.2 us; the launch traced here: 51.1 us
  Pallas kernels  50.4 us (98%)
  local copies, waits for them, and re-layouts  0.68 us (1%)
    pallas_call x1, Pallas kernels, local(): pl.pallas_call(functools.partial(kernel, groups, peers), out_shape=jax.Sh...  50.4 us

profile of v7, /device:TPU:1, one launch (start us, length us, event | category | flops | bytes accessed | tf_op | source)
XLA Modules:
  0.0 51.1 jit_solution(5932606837354276529)
XLA Ops:
  0.0 50.4 %shard_map.55 = f32[3,8,16,128]{3,2,1,0:T(8,128)S(1)} custom-call(s32[8,16]{1,0:T(8,128)} %cols_hbm.1, s32[8]{0:T(128)} %count_hbm.1, s32[2,32]{1,0:T(2,128)} %bitcast.3, f32[8,16,128]{2,1,0:T(8,128)} %basis_hbm.1, bf16[8,16,128,128]{3,2,1,0:T(8,128)(2,1)} %tiles_hbm.1), custom_call_target="tpu_custom_call" | custom-call | tf_op jit(solution)/shard_map/pallas_call | solution.py:378
  50.4 0.7 %copy.7 = f32[3,8,16,128]{3,2,1,0:T(8,128)} copy(f32[3,8,16,128]{3,2,1,0:T(8,128)S(1)} %shard_map.55) | data formatting | bytes 393216

commit v8 on v7

--- a/solution.py
+++ b/solution.py
@@ -265,8 +265,7 @@
         packed = jnp.sum(jnp.where(own_lane, gram, 0.0).reshape(vectors // 8, 8, side), axis=1)
         gram_far[t, group] = packed
 
-        @pl.loop(1, groups)
-        def _(step):
+        for step in sorted(range(1, groups), key=lambda step: -min(step, groups - step)):
             here = gram_far.at[t, group]
             remote(here, here, (far_sem.at[t, 0], far_sem.at[t, 1]), far_peer(step), me).start()
 

time: 51.2 us -> 51.2 us (level)
  no operation moved by 1% of the time
where the time goes in v8:
time: 51.2 us; the launch traced here: 51.1 us
  Pallas kernels  50.4 us (98%)
  local copies, waits for them, and re-layouts  0.68 us (1%)
    pallas_call x1, Pallas kernels, local(): pl.pallas_call(functools.partial(kernel, groups, peers), out_shape=jax.Sh...  50.4 us

profile of v8, /device:TPU:1, one launch (start us, length us, event | category | flops | bytes accessed | tf_op | source)
XLA Modules:
  0.0 51.1 jit_solution(9111503355981599770)
XLA Ops:
  0.0 50.4 %shard_map.55 = f32[3,8,16,128]{3,2,1,0:T(8,128)S(1)} custom-call(s32[8,16]{1,0:T(8,128)} %cols_hbm.1, s32[8]{0:T(128)} %count_hbm.1, s32[2,32]{1,0:T(2,128)} %bitcast.3, f32[8,16,128]{2,1,0:T(8,128)} %basis_hbm.1, bf16[8,16,128,128]{3,2,1,0:T(8,128)(2,1)} %tiles_hbm.1), custom_call_target="tpu_custom_call" | custom-call | tf_op jit(solution)/shard_map/pallas_call | solution.py:377
  50.4 0.7 %copy.7 = f32[3,8,16,128]{3,2,1,0:T(8,128)} copy(f32[3,8,16,128]{3,2,1,0:T(8,128)S(1)} %shard_map.55) | data formatting | bytes 393216
